TPU v7x, 32 devices: a whole 2x2x4 slice. The times are simulated.
32 devices in a mesh: tm: 8 (over y, x, core), mp: 4 (over z).
Axes of the slice: x: 2, y: 2, z: 4, core: 2. Of those that a mesh axis runs over, the one named last changes fastest.
Arguments:
- frames: bfloat16 [4096, 1024], P(('tm', 'mp')), may hold values from -6 to 6
- block_ids: int32 [4096], replicated, may hold values from 0 to 203, never falling along the last dimension, each value on 1 to 40 neighbouring positions
- valid_counts: int32 [8], replicated, may hold values from 1 to 512, as said below
- norm_attn: float32 [1024], replicated, may hold values from 0.25 to 1.75
- w_qkv: bfloat16 [1024, 3072], replicated, may hold values from -1 to 1
- w_attn_out: bfloat16 [1024, 1024], replicated, may hold values from -0.1875 to 0.1875
- norm_conv: float32 [1024], replicated, may hold values from 0.25 to 1.75
- w_point_in: bfloat16 [1024, 2048], replicated, may hold values from -0.1875 to 0.1875
- w_depth: bfloat16 [31, 1024], replicated, may hold values from -1 to 1
- w_point_out: bfloat16 [1024, 1024], replicated, may hold values from -0.1875 to 0.1875
- w_adapter: bfloat16 [1024, 8192], P('tm', 'mp'), may hold values from -1 to 1
- llm_gain: float32 [8192], replicated, may hold values from 0.25 to 1.75
- w_query: bfloat16 [8192, 8192], P('tm', 'mp'), may hold values from -1 to 1
- w_key: bfloat16 [8192, 1024], P('tm', 'mp'), may hold values from -1 to 1
- w_value: bfloat16 [8192, 1024], P('tm', 'mp'), may hold values from -0.0625 to 0.0625
Outputs:
- conf_out: bfloat16 [4096, 1024], P(('tm', 'mp'))
- attended: bfloat16 [1024, 8192], P('tm', 'mp')
Inputs may be any that keep to these rules, and one draw needn't show every extreme that they name: `block_ids`: block numbers never fall along the recording, and one block holds 1 to 40 frames. Every time shard but the last holds 512 real frames; the frames after the first valid_counts[t] of time shard t are padding.
All inputs are finite; a program needn't handle non-finite values.
Results may differ from a plain program's by a relative error of at most 0.014.
Values may be sent and summed in bfloat16 or wider, within the bound.
No kernel may reach another device: no remote copies, remote signals or barrier semaphores. Data moves between devices by JAX's collectives and lax.ppermute only.
A program may use at most 192 MiB of HBM per device.

v0:
```python
import math
import jax
import jax.numpy as jnp
from jax import lax
from jax.sharding import PartitionSpec as P

CH = 16
HDIM = 128
eps_conf = 1e-05
eps_llm = 1e-06
rope_base = 1000000.0
masked_score = -1e30


def passed_along(value, axis, by):
    length = lax.axis_size(axis)
    pairs = [(i, i + by) for i in range(length) if 0 <= i + by < length]
    return lax.ppermute(value, axis, pairs)


def shard_count(index, valid_counts, shard_len):
    shard = index // shard_len
    table = jnp.arange(valid_counts.shape[0], dtype=jnp.int32)
    hit = shard[:, None] == table[None, :]
    count = jnp.sum(jnp.where(hit, valid_counts[None, :], 0), axis=1)
    return (index - shard * shard_len, count)


def layer_norm(field, gain):
    center = field - jnp.mean(field, axis=-1, keepdims=True)
    spread = jnp.mean(center * center, axis=-1, keepdims=True)
    return center * lax.rsqrt(spread + eps_conf) * gain


def rotary(field, positions):
    half = field.shape[-1] // 2
    freq = rope_base ** (-(jnp.arange(half, dtype=jnp.float32) * 2.0) / field.shape[-1])
    angle = positions.astype(jnp.float32)[:, None] * freq[None, :]
    cosine = jnp.concatenate([jnp.cos(angle), jnp.cos(angle)], axis=-1)[:, None, :]
    sine = jnp.concatenate([jnp.sin(angle), jnp.sin(angle)], axis=-1)[:, None, :]
    turned = jnp.concatenate([-field[..., half:], field[..., :half]], axis=-1)
    return field * cosine + turned * sine


def on_device(
    frames,
    block_ids,
    valid_counts,
    norm_attn,
    w_qkv,
    w_attn_out,
    norm_conv,
    w_point_in,
    w_depth,
    w_point_out,
    w_adapter,
    llm_gain,
    w_query,
    w_key,
    w_value,
):
    mp_count = lax.axis_size("mp")
    frame_rows, width = frames.shape
    heads = CH
    head_size = width // heads
    shard_frames = frame_rows * mp_count
    time_place = lax.axis_index("tm")
    model_place = lax.axis_index("mp")
    first = (time_place * mp_count + model_place) * frame_rows
    inputs = frames.astype(jnp.float32)
    own_index = first + jnp.arange(frame_rows, dtype=jnp.int32)
    own_place, own_count = shard_count(own_index, valid_counts, shard_frames)
    frame_real = own_place < own_count
    normed = layer_norm(inputs, norm_attn).astype(jnp.bfloat16)
    projected = jnp.dot(normed, w_qkv, preferred_element_type=jnp.float32).astype(jnp.bfloat16)
    queries = projected[:, :width]
    own_keys = projected[:, width : 2 * width]
    own_values = projected[:, 2 * width :]
    prior_keys, prior_values = passed_along((own_keys, own_values), ("tm", "mp"), 1)
    keys = jnp.concatenate([prior_keys, own_keys], axis=0).reshape(2 * frame_rows, heads, head_size)
    values = jnp.concatenate([prior_values, own_values], axis=0).reshape(
        2 * frame_rows, heads, head_size
    )
    key_index = first - frame_rows + jnp.arange(2 * frame_rows, dtype=jnp.int32)
    key_place, key_count = shard_count(key_index, valid_counts, shard_frames)
    key_real = key_place < key_count
    prior_ids = lax.dynamic_slice_in_dim(
        block_ids, jnp.maximum(first - frame_rows, 0), frame_rows, 0
    )
    query_ids = lax.dynamic_slice_in_dim(block_ids, first, frame_rows, 0)
    key_ids = jnp.concatenate([prior_ids, query_ids], axis=0)
    same = key_index[None, :] == own_index[:, None]
    visible = (
        (key_index[None, :] <= own_index[:, None])
        & (key_ids[None, :] >= query_ids[:, None] - 2)
        & (key_real[None, :] | same)
    )
    query_heads = queries.reshape(frame_rows, heads, head_size)
    scores = jnp.einsum(
        "qhd,khd->hqk", query_heads, keys, preferred_element_type=jnp.float32
    ) / jnp.sqrt(jnp.float32(head_size))
    scores = jnp.where(visible[None], scores, masked_score)
    top = jnp.max(scores, axis=-1, keepdims=True)
    weights = jnp.where(visible[None], jnp.exp(scores - top), 0.0)
    total = jnp.sum(weights, axis=-1)
    summed = jnp.einsum(
        "hqk,khd->qhd", weights.astype(jnp.bfloat16), values, preferred_element_type=jnp.float32
    )
    conf_context = (
        (summed / jnp.transpose(total)[:, :, None]).reshape(frame_rows, width).astype(jnp.bfloat16)
    )
    mid = inputs + jnp.dot(conf_context, w_attn_out, preferred_element_type=jnp.float32)
    conv_in = layer_norm(mid, norm_conv).astype(jnp.bfloat16)
    both = jnp.dot(conv_in, w_point_in, preferred_element_type=jnp.float32)
    glu = both[:, :width] * jax.nn.sigmoid(both[:, width:])
    glu = jnp.where(frame_real[:, None], glu, 0.0).astype(jnp.bfloat16)
    taps = w_depth.shape[0]
    rim = passed_along(glu[frame_rows - (taps - 1) :], ("tm", "mp"), 1)
    padded = jnp.concatenate([rim, glu], axis=0).astype(jnp.float32)
    kernel = w_depth.astype(jnp.float32)
    depth = jnp.zeros((frame_rows, width), jnp.float32)
    for tap in range(taps):
        depth = depth + kernel[tap][None, :] * padded[taps - 1 - tap : taps - 1 - tap + frame_rows]
    activated = jax.nn.silu(depth).astype(jnp.bfloat16)
    final = mid + jnp.dot(activated, w_point_out, preferred_element_type=jnp.float32)
    conf_out = jnp.where(frame_real[:, None], final, 0.0).astype(jnp.bfloat16)
    pooled = (
        jnp.sum(conf_out.astype(jnp.float32).reshape(frame_rows // 4, 4, width), axis=1) * 0.25
    ).astype(jnp.bfloat16)
    shard_pooled = lax.all_gather(pooled, "mp", axis=0, tiled=True)
    shard_tokens = shard_pooled.shape[0]
    adapter_part = lax.all_gather(w_adapter, "tm", axis=0, tiled=True)
    adapter_full = lax.all_gather(adapter_part, "mp", axis=1, tiled=True)
    adapted = jnp.dot(shard_pooled, adapter_full, preferred_element_type=jnp.float32)
    llm_in = (
        adapted
        * lax.rsqrt(jnp.mean(adapted * adapted, axis=-1, keepdims=True) + eps_llm)
        * llm_gain
    ).astype(jnp.bfloat16)
    query_cols = w_query.shape[1]
    key_cols = w_key.shape[1]
    raw_query = jnp.dot(
        llm_in,
        lax.all_gather(w_query, "tm", axis=0, tiled=True),
        preferred_element_type=jnp.float32,
    )
    raw_keys = jnp.dot(
        llm_in, lax.all_gather(w_key, "tm", axis=0, tiled=True), preferred_element_type=jnp.float32
    )
    raw_values = jnp.dot(
        llm_in,
        lax.all_gather(w_value, "tm", axis=0, tiled=True),
        preferred_element_type=jnp.float32,
    )
    llm_size = HDIM
    query_heads_dev = query_cols // llm_size
    kv_heads = key_cols // llm_size
    group = query_heads_dev // kv_heads
    token_index = time_place * shard_tokens + jnp.arange(shard_tokens, dtype=jnp.int32)
    llm_query = rotary(
        raw_query.reshape(shard_tokens, query_heads_dev, llm_size), token_index
    ).astype(jnp.bfloat16)
    llm_query = llm_query.reshape(shard_tokens, kv_heads, group, llm_size)
    llm_keys = (
        rotary(raw_keys.reshape(shard_tokens, kv_heads, llm_size), token_index)
        .astype(jnp.bfloat16)
        .reshape(shard_tokens, key_cols)
    )
    llm_values = raw_values.astype(jnp.bfloat16)
    score_scale = 1.0 / jnp.sqrt(jnp.float32(llm_size))
    start_state = (
        jnp.full((kv_heads, group, shard_tokens), masked_score, jnp.float32),
        jnp.zeros((kv_heads, group, shard_tokens), jnp.float32),
        jnp.zeros((kv_heads, group, shard_tokens, llm_size), jnp.float32),
    )
    key_piece = lax.all_gather(llm_keys, "tm", axis=0, tiled=True)
    value_piece = lax.all_gather(llm_values, "tm", axis=0, tiled=True)
    piece_rows = key_piece.shape[0]
    step_rows = math.gcd(piece_rows, 512)

    def one_step(block, state):
        best, total_weight, accum = state
        key_block = lax.dynamic_slice_in_dim(key_piece, block * step_rows, step_rows, 0).reshape(
            step_rows, kv_heads, llm_size
        )
        value_block = lax.dynamic_slice_in_dim(
            value_piece, block * step_rows, step_rows, 0
        ).reshape(step_rows, kv_heads, llm_size)
        block_index = block * step_rows + jnp.arange(step_rows, dtype=jnp.int32)
        block_place, block_count = shard_count(block_index, valid_counts, shard_tokens)
        block_real = block_place * 4 < block_count
        matches = block_index[None, :] == token_index[:, None]
        seen = (block_index[None, :] <= token_index[:, None]) & (block_real[None, :] | matches)
        block_scores = (
            jnp.einsum("qhgd,khd->hgqk", llm_query, key_block, preferred_element_type=jnp.float32)
            * score_scale
        )
        block_scores = jnp.where(seen[None, None], block_scores, masked_score)
        new_best = jnp.maximum(best, jnp.max(block_scores, axis=-1))
        block_weights = jnp.where(
            seen[None, None], jnp.exp(block_scores - new_best[..., None]), 0.0
        )
        fade = jnp.exp(best - new_best)
        total_weight = total_weight * fade + jnp.sum(block_weights, axis=-1)
        accum = accum * fade[..., None] + jnp.einsum(
            "hgqk,khd->hgqd",
            block_weights.astype(jnp.bfloat16),
            value_block,
            preferred_element_type=jnp.float32,
        )
        return (new_best, total_weight, accum)

    best, total_weight, accum = lax.fori_loop(0, piece_rows // step_rows, one_step, start_state)
    result = accum / total_weight[..., None]
    attended = (
        jnp.transpose(result, (2, 0, 1, 3)).reshape(shard_tokens, query_cols).astype(jnp.bfloat16)
    )
    return (conf_out, attended)


def solution(mesh):
    placed = (
        P(("tm", "mp"), None),
        P(),
        P(),
        P(),
        P(),
        P(),
        P(),
        P(),
        P(),
        P(),
        P("tm", "mp"),
        P(),
        P("tm", "mp"),
        P("tm", "mp"),
        P("tm", "mp"),
    )
    return jax.shard_map(
        on_device,
        mesh=mesh,
        in_specs=placed,
        out_specs=(P(("tm", "mp"), None), P("tm", "mp")),
        check_vma=False,
    )
```

profile of v0, /device:TPU:0, one launch (start us, length us, event | category | flops | bytes accessed | tf_op | source)
XLA Modules:
  0.0 644.8 jit_solution(2328061743884182033)
XLA Ops:
  8.0 41.4 %all-gather.6.cloned.1.call-done = bf16[1024,2048]{1,0:T(8,128)(2,1)} async-done(((bf16[128,2048]{1,0:T(8,128)(2,1)}), bf16[1024,2048]{1,0:T(8,128)(2,1)}) %all-gather.6.cloned.1.call-update) | async-done | bytes 4194320 | tf_op jit(solution)/shard_map/all_gather | solution.py:132
  51.7 3.9 convolution_convert_fusion
  56.3 3.4 collective-permute-start.1
  59.7 4.1 collective-permute-start
  69.6 10.4 %collective-permute-done = bf16[128,1024]{1,0:T(8,128)(2,1)} collective-permute-done((bf16[128,1024]{1,0:T(8,128)(2,1)}, bf16[128,1024]{1,0:T(8,128)(2,1)}, u32[]{:S(2)}, u32[]{:S(2)}) %collective-permute-start) | collective-permute-done | bytes 262176 | tf_op jit(solution)/shard_map/ppermute | solution.py:18
  86.0 3.9 fusion.22
  91.0 3.1 fusion.72
  94.3 13.2 %collective-permute-start.2 = (bf16[30,1024]{1,0:T(8,128)(2,1)S(1)}, bf16[30,1024]{1,0:T(8,128)(2,1)S(1)}, u32[]{:S(2)}, u32[]{:S(2)}) collective-permute-start(bf16[30,1024]{1,0:T(8,128)(2,1)S(1)} %slice.294), channel_id=1, source_target_pairs={{0,1},{1,2},{2,3},{3,4},{4,5},{5,6},{6,7},{7,8},{8,9},{9,10},{10,1... | collective-permute-start | bytes 184328 | tf_op jit(solution)/shard_map/ppermute | solution.py:18
  107.6 3.0 collective-permute-done.2
  114.1 36.5 %all_gather.24 = bf16[128,1024]{1,0:T(8,128)(2,1)S(1)} all-gather(bf16[32,1024]{1,0:T(8,128)(2,1)S(1)} %multiply_convert_fusion.5), channel_id=1, replica_groups=mesh['tm'=8,'mp'=4] {'mp'}, dimensions={0}, use_global_device_ids=true | all-gather | bytes 327680 | tf_op jit(solution)/shard_map/all_gather | solution.py:130
  150.6 200.2 %all-gather.8.cloned.1.call-done = bf16[1024,8192]{1,0:T(8,128)(2,1)} async-done(((bf16[1024,2048]{1,0:T(8,128)(2,1)}), bf16[1024,8192]{1,0:T(8,128)(2,1)}) %all-gather.8.cloned.1.call-update) | async-done | bytes 16777232 | tf_op jit(solution)/shard_map/all_gather | solution.py:133
  350.8 8.2 %multiply_reduce_fusion = (f32[128]{0:T(128)S(1)}, f32[128,8192]{1,0:T(8,128)S(1)}) fusion(bf16[128,1024]{1,0:T(8,128)(2,1)S(1)} %all_gather.24, bf16[1024,8192]{1,0:T(8,128)(2,1)} %all-gather.8.cloned.1.call-done), kind=kOutput, calls=%fused_computation.35 | convolution fusion | flops 2149580800 | bytes 21234176 | tf_op jit(solution)/shard_map/dot_general | solution.py:134
  359.5 27.4 %all-gather.10.cloned.1.call-done = bf16[8192,256]{1,0:T(8,128)(2,1)} async-done(((bf16[1024,256]{1,0:T(8,128)(2,1)}), bf16[8192,256]{1,0:T(8,128)(2,1)}) %all-gather.10.cloned.1.call-update) | async-done | bytes 4194320 | tf_op jit(solution)/shard_map/all_gather | solution.py:148
  390.4 12.2 %all_gather.28 = bf16[1024,256]{1,0:T(8,128)(2,1)} all-gather(bf16[128,256]{1,0:T(8,128)(2,1)S(1)} %fusion.82), channel_id=1, replica_groups=mesh['tm'=8,'mp'=4] {'tm'}, dimensions={0}, use_global_device_ids=true | all-gather | bytes 589824 | tf_op jit(solution)/shard_map/all_gather | solution.py:176
  402.6 23.5 %all-gather.14.cloned.1.call-done = bf16[8192,256]{1,0:T(8,128)(2,1)} async-done(((bf16[1024,256]{1,0:T(8,128)(2,1)}), bf16[8192,256]{1,0:T(8,128)(2,1)}) %all-gather.14.cloned.1.call-update) | async-done | bytes 4194320 | tf_op jit(solution)/shard_map/all_gather | solution.py:152
  426.1 2.9 convolution_convert_fusion.1
  429.0 10.8 %all_gather.31 = bf16[1024,256]{1,0:T(8,128)(2,1)} all-gather(bf16[128,256]{1,0:T(8,128)(2,1)S(1)} %convolution_convert_fusion.1), channel_id=1, replica_groups=mesh['tm'=8,'mp'=4] {'tm'}, dimensions={0}, use_global_device_ids=true | all-gather | bytes 589824 | tf_op jit(solution)/shard_map/all_gather | solution.py:177
  439.8 148.9 %all-gather.12.cloned.1.call-done = bf16[8192,2048]{1,0:T(8,128)(2,1)} async-done(((bf16[1024,2048]{1,0:T(8,128)(2,1)}), bf16[8192,2048]{1,0:T(8,128)(2,1)}) %all-gather.12.cloned.1.call-update) | async-done | bytes 33554448 | tf_op jit(solution)/shard_map/all_gather | solution.py:144
  588.7 12.9 %fusion.99 = f32[128,2048]{1,0:T(8,128)S(1)} fusion(bf16[128,8192]{1,0:T(8,128)(2,1)S(1)} %multiply_convert_fusion, bf16[8192,2048]{1,0:T(8,128)(2,1)} %all-gather.12.cloned.1.call-done), kind=kOutput, calls=%fused_computation.199 | convolution fusion | flops 4294967296 | bytes 36700160 | tf_op jit(solution)/shard_map/dot_general | solution.py:142
  610.2 25.0 %while.20 = (s32[]{:T(128)}, f32[2,8,128]{2,1,0:T(8,128)S(1)}, f32[2,8,128]{2,1,0:T(8,128)S(1)}, f32[2,8,128,128]{3,2,1,0:T(8,128)}, s32[8]{0:T(128)S(1)}, /*ind...) while((s32[]{:T(128)}, f32[2,8,128]{2,1,0:T(8,128)S(1)}, ...), condition=%wide.region_14.15_spmd.clone, body=%wide.region_10.14_spmd.clone.sunk | while | flops 551591552 | bytes 26622240 | solution.py:213
  614.6 3.2 fusion.134
  617.9 3.9 fusion.136
  627.1 3.2 fusion.134
  630.4 3.9 fusion.136
  (192 shorter events, 46.0 us)
Async XLA Ops:
  7.2 82.7 %copy-start = (bf16[1024,1024]{1,0:T(8,128)(2,1)S(1)}, bf16[1024,1024]{1,0:T(8,128)(2,1)}, u32[]{:S(2)}) copy-start(bf16[1024,1024]{1,0:T(8,128)(2,1)} %param.22) | copy-start | bytes 6291460
  7.2 42.2 %all-gather.6.cloned.1.call-start = ((), (), s32[]{:S(2)}) async-start(), calls=%async_computation | async-start | bytes 4718592 | tf_op jit(solution)/shard_map/all_gather | solution.py:132
  7.9 342.8 %all-gather.8.cloned.1.call-start = ((), (), s32[]{:S(2)}) async-start(), calls=%async_computation.1 | async-start | bytes 20971520 | tf_op jit(solution)/shard_map/all_gather | solution.py:133
  49.4 337.5 %all-gather.10.cloned.1.call-start = ((), (), s32[]{:S(2)}) async-start(), calls=%async_computation.2 | async-start | bytes 4718592 | tf_op jit(solution)/shard_map/all_gather | solution.py:148
  50.1 376.0 %all-gather.14.cloned.1.call-start = ((), (), s32[]{:S(2)}) async-start(), calls=%async_computation.4 | async-start | bytes 4718592 | tf_op jit(solution)/shard_map/all_gather | solution.py:152
  50.7 538.0 %all-gather.12.cloned.1.call-start = ((), (), s32[]{:S(2)}) async-start(), calls=%async_computation.3 | async-start | bytes 37748736 | tf_op jit(solution)/shard_map/all_gather | solution.py:144
  56.3 13.0 %collective-permute-start.1 = (bf16[128,1024]{1,0:T(8,128)(2,1)S(1)}, bf16[128,1024]{1,0:T(8,128)(2,1)S(1)}, u32[]{:S(2)}, u32[]{:S(2)}) collective-permute-start(bf16[128,1024]{1,0:T(8,128)(2,1)S(1)} %get-tuple-element.316), channel_id=1, source_target_pairs={{0,1},{1,2},{2,3},{3,4},{4,5},{5,6},{6,7},{7,8},{8,9},{9,10},{10,1... | collective-permute-start | bytes 786440 | tf_op jit(solution)/shard_map/ppermute | solution.py:18
  59.7 20.3 %collective-permute-start = (bf16[128,1024]{1,0:T(8,128)(2,1)}, bf16[128,1024]{1,0:T(8,128)(2,1)}, u32[]{:S(2)}, u32[]{:S(2)}) collective-permute-start(bf16[128,1024]{1,0:T(8,128)(2,1)} %get-tuple-element.318), channel_id=1, source_target_pairs={{0,1},{1,2},{2,3},{3,4},{4,5},{5,6},{6,7},{7,8},{8,9},{9,10},{10,1... | collective-permute-start | bytes 786440 | tf_op jit(solution)/shard_map/ppermute | solution.py:18
  90.6 20.1 %copy-start.13 = (f32[1,1024]{1,0:T(1,128)S(1)}, f32[1,1024]{1,0:T(1,128)}, u32[]{:S(2)}) copy-start(f32[1,1024]{1,0:T(1,128)} %get-tuple-element.340) | copy-start | bytes 12292
  90.7 20.1 %copy-start.14 = (f32[1,1024]{1,0:T(1,128)S(1)}, f32[1,1024]{1,0:T(1,128)}, u32[]{:S(2)}) copy-start(f32[1,1024]{1,0:T(1,128)} %get-tuple-element.341) | copy-start | bytes 12292
  90.7 20.1 %copy-start.15 = (f32[1,1024]{1,0:T(1,128)S(1)}, f32[1,1024]{1,0:T(1,128)}, u32[]{:S(2)}) copy-start(f32[1,1024]{1,0:T(1,128)} %get-tuple-element.342) | copy-start | bytes 12292
  90.7 20.1 %copy-start.16 = (f32[1,1024]{1,0:T(1,128)S(1)}, f32[1,1024]{1,0:T(1,128)}, u32[]{:S(2)}) copy-start(f32[1,1024]{1,0:T(1,128)} %get-tuple-element.343) | copy-start | bytes 12292
  90.7 20.1 %copy-start.17 = (f32[1,1024]{1,0:T(1,128)S(1)}, f32[1,1024]{1,0:T(1,128)}, u32[]{:S(2)}) copy-start(f32[1,1024]{1,0:T(1,128)} %get-tuple-element.344) | copy-start | bytes 12292
  90.7 20.1 %copy-start.18 = (f32[1,1024]{1,0:T(1,128)S(1)}, f32[1,1024]{1,0:T(1,128)}, u32[]{:S(2)}) copy-start(f32[1,1024]{1,0:T(1,128)} %get-tuple-element.345) | copy-start | bytes 12292
  90.7 20.1 %copy-start.19 = (f32[1,1024]{1,0:T(1,128)S(1)}, f32[1,1024]{1,0:T(1,128)}, u32[]{:S(2)}) copy-start(f32[1,1024]{1,0:T(1,128)} %get-tuple-element.346) | copy-start | bytes 12292
  90.7 20.1 %copy-start.20 = (f32[1,1024]{1,0:T(1,128)S(1)}, f32[1,1024]{1,0:T(1,128)}, u32[]{:S(2)}) copy-start(f32[1,1024]{1,0:T(1,128)} %get-tuple-element.347) | copy-start | bytes 12292
  90.7 20.1 %copy-start.21 = (f32[1,1024]{1,0:T(1,128)S(1)}, f32[1,1024]{1,0:T(1,128)}, u32[]{:S(2)}) copy-start(f32[1,1024]{1,0:T(1,128)} %get-tuple-element.348) | copy-start | bytes 12292
  90.7 20.1 %copy-start.22 = (f32[1,1024]{1,0:T(1,128)S(1)}, f32[1,1024]{1,0:T(1,128)}, u32[]{:S(2)}) copy-start(f32[1,1024]{1,0:T(1,128)} %get-tuple-element.349) | copy-start | bytes 12292
  90.7 20.1 %copy-start.23 = (f32[1,1024]{1,0:T(1,128)S(1)}, f32[1,1024]{1,0:T(1,128)}, u32[]{:S(2)}) copy-start(f32[1,1024]{1,0:T(1,128)} %get-tuple-element.350) | copy-start | bytes 12292
  90.8 20.1 %copy-start.24 = (f32[1,1024]{1,0:T(1,128)S(1)}, f32[1,1024]{1,0:T(1,128)}, u32[]{:S(2)}) copy-start(f32[1,1024]{1,0:T(1,128)} %get-tuple-element.351) | copy-start | bytes 12292
  90.8 20.1 %copy-start.25 = (f32[1,1024]{1,0:T(1,128)S(1)}, f32[1,1024]{1,0:T(1,128)}, u32[]{:S(2)}) copy-start(f32[1,1024]{1,0:T(1,128)} %get-tuple-element.321) | copy-start | bytes 12292
  94.3 16.3 %collective-permute-start.2 = (bf16[30,1024]{1,0:T(8,128)(2,1)S(1)}, bf16[30,1024]{1,0:T(8,128)(2,1)S(1)}, u32[]{:S(2)}, u32[]{:S(2)}) collective-permute-start(bf16[30,1024]{1,0:T(8,128)(2,1)S(1)} %slice.294), channel_id=1, source_target_pairs={{0,1},{1,2},{2,3},{3,4},{4,5},{5,6},{6,7},{7,8},{8,9},{9,10},{10,1... | collective-permute-start | bytes 184328 | tf_op jit(solution)/shard_map/ppermute | solution.py:18
  113.6 245.4 %copy-start.7 = (bf16[128,1024]{1,0:T(8,128)(2,1)}, bf16[128,1024]{1,0:T(8,128)(2,1)S(1)}, u32[]{:S(2)}) copy-start(bf16[128,1024]{1,0:T(8,128)(2,1)S(1)} %fusion.23) | copy-start | bytes 786436
  150.6 208.4 %copy-start.10 = (f32[8192]{0:T(1024)S(1)}, f32[8192]{0:T(1024)}, u32[]{:S(2)}) copy-start(f32[8192]{0:T(1024)} %param.28) | copy-start | bytes 98308
  (33 other events, 455.9 us)
Sparse Core Ops, SparseCore 0:
  9.9 39.4 all-gather.5
  50.9 299.7 all-gather.7
  352.7 34.2 all-gather.9
  388.7 37.3 all-gather.13
  427.8 160.7 all-gather.11
where the time goes:
time: 646 us; the launch traced here: 645 us
  waiting for transfers between devices  458 us (71%)
  blocking collectives  59.4 us (9%)
  matrix products  58.1 us (9%)
  starting transfers between devices  20.9 us (3%)
  other arithmetic  18.1 us (3%)
  local copies, waits for them, and re-layouts  15.7 us (2%)
  between operations  14.7 us (2%)
    all_gather x1, waiting for transfers between devices, on_device(): adapter_full = lax.all_gather(adapter_part, 'mp', axis=1, tiled=True)  200 us
    all_gather x1, waiting for transfers between devices, on_device(): lax.all_gather(w_query, 'tm', axis=0, tiled=True)  149 us
    all_gather x1, waiting for transfers between devices, on_device(): adapter_part = lax.all_gather(w_adapter, 'tm', axis=0, tiled=True)  41.4 us
    all_gather x1, blocking collectives, on_device(): shard_pooled = lax.all_gather(pooled, 'mp', axis=0, tiled=True)  36.5 us
    all_gather x1, waiting for transfers between devices, on_device(): lax.all_gather(w_key, 'tm', axis=0, tiled=True)  27.4 us
    all_gather x1, waiting for transfers between devices, on_device(): lax.all_gather(w_value, 'tm', axis=0, tiled=True)  23.5 us
    ppermute x3, starting transfers between devices, passed_along(): return lax.ppermute(value, axis, pairs)  20.7 us
    ppermute x3, waiting for transfers between devices, passed_along(): return lax.ppermute(value, axis, pairs)  14.1 us
  transfers between devices with their start and end apart: 8, of which 8 were waited for; matrix products, arithmetic and copies ran while one was open for 7% of the time, Pallas kernels for 0%

commit v1 on v0

--- a/solution.py
+++ b/solution.py
@@ -173,8 +173,11 @@
         jnp.zeros((kv_heads, group, shard_tokens), jnp.float32),
         jnp.zeros((kv_heads, group, shard_tokens, llm_size), jnp.float32),
     )
-    key_piece = lax.all_gather(llm_keys, "tm", axis=0, tiled=True)
-    value_piece = lax.all_gather(llm_values, "tm", axis=0, tiled=True)
+    key_piece, value_piece = jnp.split(
+        lax.all_gather(jnp.concatenate([llm_keys, llm_values], axis=1), "tm", axis=0, tiled=True),
+        [llm_keys.shape[1]],
+        axis=1,
+    )
     piece_rows = key_piece.shape[0]
     step_rows = math.gcd(piece_rows, 512)
 

time: 646 us -> 671 us (1.039)
  waiting for transfers between devices: 458 us -> 514 us
  blocking collectives: 59.4 us -> 25.4 us
    all_gather x0 -> x1, waiting for transfers between devices: none -> 23 us  [on_device(): lax.all_gather(jnp.concatenate([llm_keys, llm_values], axis=1), 'tm', axi...]
    all_gather x2 -> x0, blocking collectives: 23 us -> none  [the longest x1 12.2 us: on_device(): key_piece = lax.all_gather(llm_keys, 'tm', axis=0, tiled=True)]
    all_gather x1, waiting for transfers between devices: 200 us -> 216 us  [on_device(): adapter_full = lax.all_gather(adapter_part, 'mp', axis=1, tiled=True)]
    all_gather x1, waiting for transfers between devices: 149 us -> 160 us  [on_device(): lax.all_gather(w_query, 'tm', axis=0, tiled=True)]
    all_gather x1, waiting for transfers between devices: 23.5 us -> 35 us  [on_device(): lax.all_gather(w_value, 'tm', axis=0, tiled=True)]
    all_gather x1, blocking collectives: 36.5 us -> 25.4 us  [on_device(): shard_pooled = lax.all_gather(pooled, 'mp', axis=0, tiled=True)]
  transfers between devices with their start and end apart: 8 -> 9, of which waited for: 8 -> 8; matrix products, arithmetic and copies ran while one was open for 7% -> 6% of each run, Pallas kernels for 0% -> 0%
where the time goes in v1:
time: 671 us
  waiting for transfers between devices  514 us (77%)
  matrix products  59.6 us (9%)
  blocking collectives  25.4 us (4%)
  starting transfers between devices  21 us (3%)
  other arithmetic  18.2 us (3%)
  local copies, waits for them, and re-layouts  17.2 us (3%)
  between operations  15.1 us (2%)
    all_gather x1, waiting for transfers between devices, on_device(): adapter_full = lax.all_gather(adapter_part, 'mp', axis=1, tiled=True)  216 us
    all_gather x1, waiting for transfers between devices, on_device(): lax.all_gather(w_query, 'tm', axis=0, tiled=True)  160 us
    all_gather x1, waiting for transfers between devices, on_device(): adapter_part = lax.all_gather(w_adapter, 'tm', axis=0, tiled=True)  41.4 us
    all_gather x1, waiting for transfers between devices, on_device(): lax.all_gather(w_value, 'tm', axis=0, tiled=True)  35 us
    all_gather x1, waiting for transfers between devices, on_device(): lax.all_gather(w_key, 'tm', axis=0, tiled=True)  27.3 us
    all_gather x1, blocking collectives, on_device(): shard_pooled = lax.all_gather(pooled, 'mp', axis=0, tiled=True)  25.4 us
    all_gather x1, waiting for transfers between devices, on_device(): lax.all_gather(jnp.concatenate([llm_keys, llm_values], axis=1), 'tm', axi...  23 us
    ppermute x3, starting transfers between devices, passed_along(): return lax.ppermute(value, axis, pairs)  20.8 us
  transfers between devices with their start and end apart: 9, of which 8 were waited for; matrix products, arithmetic and copies ran while one was open for 6% of the time, Pallas kernels for 0%

profile of v1, /device:TPU:0, one launch (start us, length us, event | category | flops | bytes accessed | tf_op | source)
XLA Modules:
  0.0 670.6 jit_solution(2148825326402051639)
XLA Ops:
  8.0 41.4 %all-gather.7.cloned.1.call-done = bf16[1024,2048]{1,0:T(8,128)(2,1)} async-done(((bf16[128,2048]{1,0:T(8,128)(2,1)}), bf16[1024,2048]{1,0:T(8,128)(2,1)}) %all-gather.7.cloned.1.call-update) | async-done | bytes 4194320 | tf_op jit(solution)/shard_map/all_gather | solution.py:132
  50.6 3.9 convolution_convert_fusion
  55.2 3.4 collective-permute-start.1
  58.6 4.1 collective-permute-start
  72.2 5.5 collective-permute-done
  79.1 3.8 fusion.22
  84.0 3.1 fusion.72
  87.3 13.3 %collective-permute-start.2 = (bf16[30,1024]{1,0:T(8,128)(2,1)S(1)}, bf16[30,1024]{1,0:T(8,128)(2,1)S(1)}, u32[]{:S(2)}, u32[]{:S(2)}) collective-permute-start(bf16[30,1024]{1,0:T(8,128)(2,1)S(1)} %slice.294), channel_id=1, source_target_pairs={{0,1},{1,2},{2,3},{3,4},{4,5},{5,6},{6,7},{7,8},{8,9},{9,10},{10,1... | collective-permute-start | bytes 184328 | tf_op jit(solution)/shard_map/ppermute | solution.py:18
  100.7 3.0 collective-permute-done.2
  104.1 3.2 fusion.23
  107.9 25.4 %all_gather.21 = bf16[128,1024]{1,0:T(8,128)(2,1)S(1)} all-gather(bf16[32,1024]{1,0:T(8,128)(2,1)S(1)} %multiply_convert_fusion.5), channel_id=1, replica_groups=mesh['tm'=8,'mp'=4] {'mp'}, dimensions={0}, use_global_device_ids=true | all-gather | bytes 327680 | tf_op jit(solution)/shard_map/all_gather | solution.py:130
  133.3 216.4 %all-gather.9.cloned.1.call-done = bf16[1024,8192]{1,0:T(8,128)(2,1)} async-done(((bf16[1024,2048]{1,0:T(8,128)(2,1)}), bf16[1024,8192]{1,0:T(8,128)(2,1)}) %all-gather.9.cloned.1.call-update) | async-done | bytes 16777232 | tf_op jit(solution)/shard_map/all_gather | solution.py:133
  349.7 8.2 %multiply_reduce_fusion = (f32[128]{0:T(128)S(1)}, f32[128,8192]{1,0:T(8,128)S(1)}) fusion(bf16[128,1024]{1,0:T(8,128)(2,1)S(1)} %all_gather.21, bf16[1024,8192]{1,0:T(8,128)(2,1)} %all-gather.9.cloned.1.call-done), kind=kOutput, calls=%fused_computation.35 | convolution fusion | flops 2149580800 | bytes 21234176 | tf_op jit(solution)/shard_map/dot_general | solution.py:134
  358.4 27.3 %all-gather.11.cloned.1.call-done = bf16[8192,256]{1,0:T(8,128)(2,1)} async-done(((bf16[1024,256]{1,0:T(8,128)(2,1)}), bf16[8192,256]{1,0:T(8,128)(2,1)}) %all-gather.11.cloned.1.call-update) | async-done | bytes 4194320 | tf_op jit(solution)/shard_map/all_gather | solution.py:148
  389.3 35.0 %all-gather.13.cloned.1.call-done = bf16[8192,256]{1,0:T(8,128)(2,1)} async-done(((bf16[1024,256]{1,0:T(8,128)(2,1)}), bf16[8192,256]{1,0:T(8,128)(2,1)}) %all-gather.13.cloned.1.call-update) | async-done | bytes 4194320 | tf_op jit(solution)/shard_map/all_gather | solution.py:152
  424.3 2.9 convolution_convert_fusion.1
  428.5 23.0 %all-gather.15.cloned.1.call-done = bf16[1024,512]{1,0:T(8,128)(2,1)} async-done(((bf16[128,512]{1,0:T(8,128)(2,1)}), bf16[1024,512]{1,0:T(8,128)(2,1)}) %all-gather.15.cloned.1.call-update) | async-done | bytes 1048592 | tf_op jit(solution)/shard_map/all_gather | solution.py:177
  453.7 160.3 %all-gather.17.cloned.1.call-done = bf16[8192,2048]{1,0:T(8,128)(2,1)} async-done(((bf16[1024,2048]{1,0:T(8,128)(2,1)}), bf16[8192,2048]{1,0:T(8,128)(2,1)}) %all-gather.17.cloned.1.call-update) | async-done | bytes 33554448 | tf_op jit(solution)/shard_map/all_gather | solution.py:144
  614.1 12.9 %fusion.100 = f32[128,2048]{1,0:T(8,128)S(1)} fusion(bf16[128,8192]{1,0:T(8,128)(2,1)S(1)} %multiply_convert_fusion, bf16[8192,2048]{1,0:T(8,128)(2,1)} %all-gather.17.cloned.1.call-done), kind=kOutput, calls=%fused_computation.201 | convolution fusion | flops 4294967296 | bytes 36700160 | tf_op jit(solution)/shard_map/dot_general | solution.py:142
  635.7 25.1 %while.20 = (s32[]{:T(128)}, f32[2,8,128]{2,1,0:T(8,128)S(1)}, f32[2,8,128]{2,1,0:T(8,128)S(1)}, f32[2,8,128,128]{3,2,1,0:T(8,128)}, s32[8]{0:T(128)S(1)}, /*ind...) while((s32[]{:T(128)}, f32[2,8,128]{2,1,0:T(8,128)S(1)}, ...), condition=%wide.region_14.15_spmd.clone, body=%wide.region_10.14_spmd.clone.sunk | while | flops 551591552 | bytes 26622240 | solution.py:216
  640.0 3.2 fusion.135
  643.4 3.9 fusion.137
  652.5 3.2 fusion.135
  655.9 3.9 fusion.137
  (193 shorter events, 45.0 us)
Async XLA Ops:
  7.2 75.7 %copy-start = (bf16[1024,1024]{1,0:T(8,128)(2,1)S(1)}, bf16[1024,1024]{1,0:T(8,128)(2,1)}, u32[]{:S(2)}) copy-start(bf16[1024,1024]{1,0:T(8,128)(2,1)} %param.22) | copy-start | bytes 6291460
  7.2 43.0 %copy-start.3 = (bf16[128,1024]{1,0:T(8,128)(2,1)S(1)}, bf16[128,1024]{1,0:T(8,128)(2,1)}, u32[]{:S(2)}) copy-start(bf16[128,1024]{1,0:T(8,128)(2,1)} %param.17) | copy-start | bytes 786436
  7.2 43.4 %copy-start.8 = (f32[1024]{0:T(1024)S(1)}, f32[1024]{0:T(1024)}, u32[]{:S(2)}) copy-start(f32[1024]{0:T(1024)} %param.20) | copy-start | bytes 12292
  7.2 42.2 %all-gather.7.cloned.1.call-start = ((), (), s32[]{:S(2)}) async-start(), calls=%async_computation | async-start | bytes 4718592 | tf_op jit(solution)/shard_map/all_gather | solution.py:132
  7.9 341.7 %all-gather.9.cloned.1.call-start = ((), (), s32[]{:S(2)}) async-start(), calls=%async_computation.1 | async-start | bytes 20971520 | tf_op jit(solution)/shard_map/all_gather | solution.py:133
  49.4 336.4 %all-gather.11.cloned.1.call-start = ((), (), s32[]{:S(2)}) async-start(), calls=%async_computation.2 | async-start | bytes 4718592 | tf_op jit(solution)/shard_map/all_gather | solution.py:148
  50.1 374.1 %all-gather.13.cloned.1.call-start = ((), (), s32[]{:S(2)}) async-start(), calls=%async_computation.3 | async-start | bytes 4718592 | tf_op jit(solution)/shard_map/all_gather | solution.py:152
  55.2 12.0 %collective-permute-start.1 = (bf16[128,1024]{1,0:T(8,128)(2,1)S(1)}, bf16[128,1024]{1,0:T(8,128)(2,1)S(1)}, u32[]{:S(2)}, u32[]{:S(2)}) collective-permute-start(bf16[128,1024]{1,0:T(8,128)(2,1)S(1)} %get-tuple-element.318), channel_id=1, source_target_pairs={{0,1},{1,2},{2,3},{3,4},{4,5},{5,6},{6,7},{7,8},{8,9},{9,10},{10,1... | collective-permute-start | bytes 786440 | tf_op jit(solution)/shard_map/ppermute | solution.py:18
  58.6 19.2 %collective-permute-start = (bf16[128,1024]{1,0:T(8,128)(2,1)}, bf16[128,1024]{1,0:T(8,128)(2,1)}, u32[]{:S(2)}, u32[]{:S(2)}) collective-permute-start(bf16[128,1024]{1,0:T(8,128)(2,1)} %get-tuple-element.320), channel_id=1, source_target_pairs={{0,1},{1,2},{2,3},{3,4},{4,5},{5,6},{6,7},{7,8},{8,9},{9,10},{10,1... | collective-permute-start | bytes 786440 | tf_op jit(solution)/shard_map/ppermute | solution.py:18
  62.8 388.8 %all-gather.15.cloned.1.call-start = ((), (), s32[]{:S(2)}) async-start(), calls=%async_computation.4 | async-start | bytes 1179648 | tf_op jit(solution)/shard_map/all_gather | solution.py:177
  64.5 22.7 %copy-start.44 = (pred[128]{0:T(512)(128)(4,1)}, pred[128]{0:T(512)(128)(4,1)S(1)}, u32[]{:S(2)}) copy-start(pred[128]{0:T(512)(128)(4,1)S(1)} %subtract_compare_fusion.1) | copy-start | bytes 388
  83.7 20.1 %copy-start.12 = (f32[1,1024]{1,0:T(1,128)S(1)}, f32[1,1024]{1,0:T(1,128)}, u32[]{:S(2)}) copy-start(f32[1,1024]{1,0:T(1,128)} %get-tuple-element.323) | copy-start | bytes 12292
  83.7 20.1 %copy-start.13 = (f32[1,1024]{1,0:T(1,128)S(1)}, f32[1,1024]{1,0:T(1,128)}, u32[]{:S(2)}) copy-start(f32[1,1024]{1,0:T(1,128)} %get-tuple-element.324) | copy-start | bytes 12292
  83.7 20.1 %copy-start.14 = (f32[1,1024]{1,0:T(1,128)S(1)}, f32[1,1024]{1,0:T(1,128)}, u32[]{:S(2)}) copy-start(f32[1,1024]{1,0:T(1,128)} %get-tuple-element.325) | copy-start | bytes 12292
  83.7 20.1 %copy-start.15 = (f32[1,1024]{1,0:T(1,128)S(1)}, f32[1,1024]{1,0:T(1,128)}, u32[]{:S(2)}) copy-start(f32[1,1024]{1,0:T(1,128)} %get-tuple-element.326) | copy-start | bytes 12292
  83.7 20.1 %copy-start.16 = (f32[1,1024]{1,0:T(1,128)S(1)}, f32[1,1024]{1,0:T(1,128)}, u32[]{:S(2)}) copy-start(f32[1,1024]{1,0:T(1,128)} %get-tuple-element.327) | copy-start | bytes 12292
  83.7 20.1 %copy-start.17 = (f32[1,1024]{1,0:T(1,128)S(1)}, f32[1,1024]{1,0:T(1,128)}, u32[]{:S(2)}) copy-start(f32[1,1024]{1,0:T(1,128)} %get-tuple-element.328) | copy-start | bytes 12292
  83.7 20.1 %copy-start.18 = (f32[1,1024]{1,0:T(1,128)S(1)}, f32[1,1024]{1,0:T(1,128)}, u32[]{:S(2)}) copy-start(f32[1,1024]{1,0:T(1,128)} %get-tuple-element.329) | copy-start | bytes 12292
  83.7 20.1 %copy-start.19 = (f32[1,1024]{1,0:T(1,128)S(1)}, f32[1,1024]{1,0:T(1,128)}, u32[]{:S(2)}) copy-start(f32[1,1024]{1,0:T(1,128)} %get-tuple-element.330) | copy-start | bytes 12292
  83.8 20.1 %copy-start.20 = (f32[1,1024]{1,0:T(1,128)S(1)}, f32[1,1024]{1,0:T(1,128)}, u32[]{:S(2)}) copy-start(f32[1,1024]{1,0:T(1,128)} %get-tuple-element.331) | copy-start | bytes 12292
  87.3 16.4 %collective-permute-start.2 = (bf16[30,1024]{1,0:T(8,128)(2,1)S(1)}, bf16[30,1024]{1,0:T(8,128)(2,1)S(1)}, u32[]{:S(2)}, u32[]{:S(2)}) collective-permute-start(bf16[30,1024]{1,0:T(8,128)(2,1)S(1)} %slice.294), channel_id=1, source_target_pairs={{0,1},{1,2},{2,3},{3,4},{4,5},{5,6},{6,7},{7,8},{8,9},{9,10},{10,1... | collective-permute-start | bytes 184328 | tf_op jit(solution)/shard_map/ppermute | solution.py:18
  107.4 250.5 %copy-start.6 = (bf16[128,1024]{1,0:T(8,128)(2,1)}, bf16[128,1024]{1,0:T(8,128)(2,1)S(1)}, u32[]{:S(2)}) copy-start(bf16[128,1024]{1,0:T(8,128)(2,1)S(1)} %fusion.23) | copy-start | bytes 786436
  133.3 224.6 %copy-start.9 = (f32[8192]{0:T(1024)S(1)}, f32[8192]{0:T(1024)}, u32[]{:S(2)}) copy-start(f32[8192]{0:T(1024)} %param.28) | copy-start | bytes 98308
  427.9 186.2 %all-gather.17.cloned.1.call-start = ((), (), s32[]{:S(2)}) async-start(), calls=%async_computation.5 | async-start | bytes 37748736 | tf_op jit(solution)/shard_map/all_gather | solution.py:144
  (33 other events, 525.6 us)
Sparse Core Ops, SparseCore 0:
  9.9 39.4 all-gather.6
  50.9 298.6 all-gather.8
  351.5 34.1 all-gather.10
  387.5 36.7 all-gather.12
  428.0 23.4 all-gather.14
  453.2 160.7 all-gather.16
